TPU v7x, 32 devices: a whole 2x2x4 slice. The times are simulated.
32 devices in a mesh: team: 2 (over x), blk: 4 (over z), head: 4 (over y, core).
Axes of the slice: x: 2, y: 2, z: 4, core: 2. Of those that a mesh axis runs over, the one named last changes fastest.
Arguments:
- queries: bfloat16 [1024, 8, 8, 128], P('blk', 'head', 'team'), may hold values from -40 to 40
- features: bfloat16 [1024, 8192], P('blk', ('team', 'head')), may hold values from -6 to 6
- adapter_down: bfloat16 [4, 8192, 64], P(None, ('team', 'head')), may hold values from -0.0625 to 0.0625
- adapter_key_up: bfloat16 [4, 64, 8, 128], P(None, None, 'head'), may hold values from -0.75 to 0.75
- adapter_value_up: bfloat16 [4, 64, 8, 128], P(None, None, 'head'), may hold values from -0.75 to 0.75
- base_key: bfloat16 [1024, 8, 128], P('blk', 'head'), may hold values from -6 to 6
- base_value: bfloat16 [1024, 8, 128], P('blk', 'head'), may hold values from -24 to 24
- prefix_key: bfloat16 [2048, 8, 128], P('blk', 'head'), may hold values from -7 to 7
- prefix_value: bfloat16 [2048, 8, 128], P('blk', 'head'), may hold values from -24 to 24
- adapter_ids: int32 [4], replicated, may hold values from 0 to 3
- block_order: int32 [4], replicated, may hold values from 0 to 15
Outputs:
- attended: bfloat16 [1024, 8, 8, 128], P('blk', 'head', 'team')
All inputs are finite; a program needn't handle non-finite values.
Results may differ from a plain program's by a relative error of at most 0.011.
Values may be sent and summed in bfloat16 or wider, within the bound.
No kernel may reach another device: no remote copies, remote signals or barrier semaphores. Data moves between devices by JAX's collectives and lax.ppermute only.
A program may use at most 64 MiB of HBM per device.

v0:
```python
import math
import jax
import jax.numpy as jnp
from jax import lax
from jax.sharding import PartitionSpec as P

NEG_FILL = -1e30


def block_length(row_count):
    for candidate in range(min(row_count, 1024), 0, -1):
        if row_count % candidate == 0:
            return candidate
    return row_count


def key_positions(row_count, shard_rows, prefix_dev, query_dev, block_order, block_count):
    row_index = jnp.arange(row_count, dtype=jnp.int32)
    holder = row_index // shard_rows
    within = row_index - holder * shard_rows
    block_ids = jnp.arange(block_count, dtype=jnp.int32)
    holder_order = jnp.sum(
        jnp.where(holder[:, None] == block_ids[None, :], block_order[None, :], 0), axis=1
    )
    later = prefix_dev * block_count + holder_order * query_dev + within - prefix_dev
    return jnp.where(within < prefix_dev, holder * prefix_dev + within, later)


def attend(running, query_rows, query_pos, key_rows, value_rows, key_pos):
    row_count = key_rows.shape[0]
    block_rows = block_length(row_count)
    key_blocks = row_count // block_rows
    kv_heads = key_rows.shape[1]
    head_dim = key_rows.shape[2]
    score_scale = 1.0 / math.sqrt(head_dim)
    latest = jnp.max(query_pos)
    key_split = key_rows.reshape((key_blocks, block_rows, kv_heads, head_dim))
    value_split = value_rows.reshape((key_blocks, block_rows, kv_heads, head_dim))
    pos_split = key_pos.reshape((key_blocks, block_rows))

    def advance(carried, block_data):
        block_keys, block_values, block_pos = block_data

        def compute(previous):
            row_max, row_sum, weighted = previous
            scores = (
                jnp.einsum(
                    "tkgd,skd->kgts", query_rows, block_keys, preferred_element_type=jnp.float32
                )
                * score_scale
            )
            visible = block_pos[None, None, None, :] <= query_pos[None, None, :, None]
            scores = jnp.where(visible, scores, NEG_FILL)
            new_max = jnp.maximum(row_max, jnp.max(scores, axis=-1))
            weights = jnp.where(visible, jnp.exp(scores - new_max[..., None]), 0.0)
            factor = jnp.exp(row_max - new_max)
            row_sum = row_sum * factor + jnp.sum(weights, axis=-1)
            product = jnp.einsum(
                "kgts,skd->kgtd",
                weights.astype(jnp.bfloat16),
                block_values,
                preferred_element_type=jnp.float32,
            )
            weighted = weighted * factor[..., None] + product
            return (new_max, row_sum, weighted)

        return (lax.cond(jnp.min(block_pos) > latest, lambda kept: kept, compute, carried), None)

    result, _ = lax.scan(advance, running, (key_split, value_split, pos_split))
    return result


def on_device(
    queries,
    features,
    adapter_down,
    adapter_key_up,
    adapter_value_up,
    base_key,
    base_value,
    prefix_key,
    prefix_value,
    adapter_ids,
    block_order,
):
    block_count = lax.axis_size("blk")
    my_block = lax.axis_index("blk")
    query_dev = queries.shape[0]
    kv_heads = queries.shape[1]
    group_dev = queries.shape[2]
    head_dim = queries.shape[3]
    prefix_dev = prefix_key.shape[0]
    rank_width = adapter_down.shape[2]
    shard_rows = prefix_dev + query_dev
    chosen = adapter_ids[my_block]
    down_rows = lax.dynamic_index_in_dim(adapter_down, chosen, 0, keepdims=False)
    partial_latent = jnp.dot(features, down_rows, preferred_element_type=jnp.float32)
    latent = lax.psum(partial_latent, ("team", "head")).astype(jnp.bfloat16)

    def expand(up_table, base_rows):
        up_rows = lax.dynamic_index_in_dim(up_table, chosen, 0, keepdims=False).reshape(
            rank_width, kv_heads * head_dim
        )
        delta = jnp.dot(latent, up_rows, preferred_element_type=jnp.float32).reshape(
            query_dev, kv_heads, head_dim
        )
        return (base_rows.astype(jnp.float32) + delta).astype(jnp.bfloat16)

    key_rows = jnp.concatenate([prefix_key, expand(adapter_key_up, base_key)], axis=0)
    value_rows = jnp.concatenate([prefix_value, expand(adapter_value_up, base_value)], axis=0)
    prefix_total = prefix_dev * block_count
    offsets = jnp.arange(query_dev, dtype=jnp.int32)
    query_pos = prefix_total + block_order[my_block] * query_dev + offsets
    initial = (
        jnp.full((kv_heads, group_dev, query_dev), NEG_FILL, jnp.float32),
        jnp.zeros((kv_heads, group_dev, query_dev), jnp.float32),
        jnp.zeros((kv_heads, group_dev, query_dev, head_dim), jnp.float32),
    )
    key_piece = lax.all_gather(key_rows, "blk", axis=0, tiled=True)
    value_piece = lax.all_gather(value_rows, "blk", axis=0, tiled=True)
    piece_pos = key_positions(
        key_piece.shape[0], shard_rows, prefix_dev, query_dev, block_order, block_count
    )
    row_max, row_sum, weighted = attend(
        initial, queries, query_pos, key_piece, value_piece, piece_pos
    )
    result = weighted / row_sum[..., None]
    return result.transpose(2, 0, 1, 3).astype(jnp.bfloat16)


def solution(mesh):
    placed = (
        P("blk", "head", "team", None),
        P("blk", ("team", "head")),
        P(None, ("team", "head"), None),
        P(None, None, "head", None),
        P(None, None, "head", None),
        P("blk", "head", None),
        P("blk", "head", None),
        P("blk", "head", None),
        P("blk", "head", None),
        P(),
        P(),
    )
    return jax.shard_map(
        on_device,
        mesh=mesh,
        in_specs=placed,
        out_specs=P("blk", "head", "team", None),
        check_vma=False,
    )
```

profile of v0, /device:TPU:0, one launch (start us, length us, event | category | flops | bytes accessed | tf_op | source)
XLA Modules:
  0.0 160.4 jit_solution(10820601032562232662)
XLA Ops:
  6.5 1.3 dynamic_slice.39
  9.8 1.2 convolution_bitcast_fusion
  11.0 26.0 %psum.7 = bf16[256,64]{0,1:T(8,128)(2,1)S(1)} all-reduce(f32[256,64]{0,1:T(8,128)S(1)} %convolution_bitcast_fusion), channel_id=1, replica_groups=mesh['team'=2,'blk'=4,'head'=4] {'team','head'}, use_global_device_ids=true, to_apply=%region_0.1 | all-reduce | flops 16384 | bytes 98304 | tf_op jit(solution)/shard_map/psum | solution.py:98
  37.0 1.0 copy.35
  38.0 0.8 constant_dynamic-slice_fusion.1
  38.8 1.1 fusion.21
  39.9 0.8 pad_maximum_fusion
  40.7 0.0 all-gather.3.cloned.1.call-update
  40.7 0.0 all-gather.5.cloned.1.call-start
  40.8 1.0 copy.38
  41.8 1.1 fusion.22
  42.9 0.8 pad_maximum_fusion.1
  43.6 0.0 all-gather.5.cloned.1.call-update
  43.7 1.2 dynamic_slice.38
  45.5 0.6 add_reduce_fusion
  46.1 1.1 copy.40
  47.2 0.8 select_reduce_fusion
  48.1 29.3 %all-gather.3.cloned.1.call-done = bf16[3072,2,128]{2,0,1:T(8,128)(2,1)} async-done(((bf16[768,2,128]{2,0,1:T(8,128)(2,1)}), bf16[3072,2,128]{2,0,1:T(8,128)(2,1)}) %all-gather.3.cloned.1.call-update) | async-done | bytes 1572880 | tf_op jit(solution)/shard_map/all_gather | solution.py:119
  77.4 1.5 copy.39
  78.9 36.0 %all-gather.5.cloned.1.call-done = bf16[3072,2,128]{2,0,1:T(8,128)(2,1)} async-done(((bf16[768,2,128]{2,0,1:T(8,128)(2,1)}), bf16[3072,2,128]{2,0,1:T(8,128)(2,1)}) %all-gather.5.cloned.1.call-update) | async-done | bytes 1572880 | tf_op jit(solution)/shard_map/all_gather | solution.py:120
  114.9 2.7 %copy.41 = bf16[3,1024,2,128]{3,1,2,0:T(8,128)(2,1)} copy(bf16[3,1024,2,128]{3,1,0,2:T(8,128)(2,1)} %bitcast.83) | data formatting | bytes 3145728
  117.6 1.0 broadcast_in_dim.56
  118.6 31.8 %while.15 = (s32[]{:T(128)}, f32[2,4,256]{2,1,0:T(4,128)S(1)}, f32[2,4,256]{2,1,0:T(4,128)S(1)}, f32[2,4,256,128]{3,2,1,0:T(8,128)}, s32[3,1024]{1,0:T(4,128)S(1...) while((s32[]{:T(128)}, f32[2,4,256]{2,1,0:T(4,128)S(1)}, ...), condition=%wide.region_9.10_spmd.clone, body=%wide.region_3.9_spmd.clone.sunk | while | flops 1101796608 | bytes 38421312 | solution.py:69
  118.6 0.6 fusion.45
  120.5 8.7 %conditional.3 = (f32[2,4,256]{2,1,0:T(4,128)S(1)}, f32[2,4,256]{2,1,0:T(4,128)S(1)}, f32[2,4,256,128]{3,2,1,0:T(8,128)}) conditional(s32[]{:T(128)} %convert_element_type.57, (s32[1,1024]{1,0:T(1,128)S(1)}, s32[]{:T(128)}, bf16[3,1024,2,128]{3,1,2,0:T(8,128)(2,1)S(1)}, s32[]{:T(128)}, bf16[256,2,4,128]{3,0,2,1:T(8,128)(2,1)S(1)}, ...), branch_computations={%region_5.7_spmd, %region_8.8_spmd} | conditional | flops 1101795584 | bytes 38395480 | solution.py:67
  120.5 0.2 broadcast_compare_fusion
  120.7 0.0 copy-start.1
  120.7 1.4 fusion.2
  122.2 2.0 %fusion.4 = f32[2,4,256]{2,1,0:T(4,128)S(1)} fusion(f32[2,1024,256,4]{2,1,3,0:T(8,128)S(1)} %get-tuple-element.228, f32[2,4,256]{2,1,0:T(4,128)S(1)} %max.4, pred[256,1024]{0,1:T(8,128)(4,1)S(1)} %broadcast_compare_fusion), kind=kLoop, calls=%fused_computation.5 | loop fusion | flops 10483712 | bytes 8667136 | tf_op jit(solution)/shard_map/while/body/eval_jaxpr/cond/branch_0_fun/reduce_sum | solution.py:57
  124.2 4.0 %fusion.8 = f32[2,4,256,128]{3,2,1,0:T(8,128)S(1)} fusion(f32[2,1024,256,4]{2,1,3,0:T(8,128)S(1)} %get-tuple-element.228, f32[2,4,256]{2,1,0:T(4,128)S(1)} %max.4, pred[256,1024]{0,1:T(8,128)(4,1)S(1)} %broadcast_compare_fusion, f32[2,4,256,128]{3,2,1,0:T(8,128)S(1)} %copy-done.1, bf16[3,1024,2,128]{3,1,2,0:T(8,128)(2,1)} %get-tuple-element.125, ...), kind=kOutput, calls=%fused_computation.8 | convolution fusion | flops 547880960 | bytes 11289088 | tf_op jit(solution)/shard_map/while/body/eval_jaxpr/cond/branch_0_fun/kgts,skd->kgtd/dot_general | solution.py:58
  128.3 1.0 copy-done.2
  129.2 0.6 fusion.45
  131.1 8.7 %conditional.3 = (f32[2,4,256]{2,1,0:T(4,128)S(1)}, f32[2,4,256]{2,1,0:T(4,128)S(1)}, f32[2,4,256,128]{3,2,1,0:T(8,128)}) conditional(s32[]{:T(128)} %convert_element_type.57, (s32[1,1024]{1,0:T(1,128)S(1)}, s32[]{:T(128)}, bf16[3,1024,2,128]{3,1,2,0:T(8,128)(2,1)S(1)}, s32[]{:T(128)}, bf16[256,2,4,128]{3,0,2,1:T(8,128)(2,1)S(1)}, ...), branch_computations={%region_5.7_spmd, %region_8.8_spmd} | conditional | flops 1101795584 | bytes 38395480 | solution.py:67
  131.1 0.2 broadcast_compare_fusion
  131.3 0.0 copy-start.1
  131.3 1.4 fusion.2
  132.8 2.0 %fusion.4 = f32[2,4,256]{2,1,0:T(4,128)S(1)} fusion(f32[2,1024,256,4]{2,1,3,0:T(8,128)S(1)} %get-tuple-element.228, f32[2,4,256]{2,1,0:T(4,128)S(1)} %max.4, pred[256,1024]{0,1:T(8,128)(4,1)S(1)} %broadcast_compare_fusion), kind=kLoop, calls=%fused_computation.5 | loop fusion | flops 10483712 | bytes 8667136 | tf_op jit(solution)/shard_map/while/body/eval_jaxpr/cond/branch_0_fun/reduce_sum | solution.py:57
  134.8 4.0 %fusion.8 = f32[2,4,256,128]{3,2,1,0:T(8,128)S(1)} fusion(f32[2,1024,256,4]{2,1,3,0:T(8,128)S(1)} %get-tuple-element.228, f32[2,4,256]{2,1,0:T(4,128)S(1)} %max.4, pred[256,1024]{0,1:T(8,128)(4,1)S(1)} %broadcast_compare_fusion, f32[2,4,256,128]{3,2,1,0:T(8,128)S(1)} %copy-done.1, bf16[3,1024,2,128]{3,1,2,0:T(8,128)(2,1)} %get-tuple-element.125, ...), kind=kOutput, calls=%fused_computation.8 | convolution fusion | flops 547880960 | bytes 11289088 | tf_op jit(solution)/shard_map/while/body/eval_jaxpr/cond/branch_0_fun/kgts,skd->kgtd/dot_general | solution.py:58
  138.9 1.0 copy-done.2
  139.8 0.6 fusion.45
  141.7 8.7 %conditional.3 = (f32[2,4,256]{2,1,0:T(4,128)S(1)}, f32[2,4,256]{2,1,0:T(4,128)S(1)}, f32[2,4,256,128]{3,2,1,0:T(8,128)}) conditional(s32[]{:T(128)} %convert_element_type.57, (s32[1,1024]{1,0:T(1,128)S(1)}, s32[]{:T(128)}, bf16[3,1024,2,128]{3,1,2,0:T(8,128)(2,1)S(1)}, s32[]{:T(128)}, bf16[256,2,4,128]{3,0,2,1:T(8,128)(2,1)S(1)}, ...), branch_computations={%region_5.7_spmd, %region_8.8_spmd} | conditional | flops 1101795584 | bytes 38395480 | solution.py:67
  141.7 0.2 broadcast_compare_fusion
  141.9 1.4 fusion.2
  143.4 2.0 %fusion.4 = f32[2,4,256]{2,1,0:T(4,128)S(1)} fusion(f32[2,1024,256,4]{2,1,3,0:T(8,128)S(1)} %get-tuple-element.228, f32[2,4,256]{2,1,0:T(4,128)S(1)} %max.4, pred[256,1024]{0,1:T(8,128)(4,1)S(1)} %broadcast_compare_fusion), kind=kLoop, calls=%fused_computation.5 | loop fusion | flops 10483712 | bytes 8667136 | tf_op jit(solution)/shard_map/while/body/eval_jaxpr/cond/branch_0_fun/reduce_sum | solution.py:57
  145.4 4.0 %fusion.8 = f32[2,4,256,128]{3,2,1,0:T(8,128)S(1)} fusion(f32[2,1024,256,4]{2,1,3,0:T(8,128)S(1)} %get-tuple-element.228, f32[2,4,256]{2,1,0:T(4,128)S(1)} %max.4, pred[256,1024]{0,1:T(8,128)(4,1)S(1)} %broadcast_compare_fusion, f32[2,4,256,128]{3,2,1,0:T(8,128)S(1)} %copy-done.1, bf16[3,1024,2,128]{3,1,2,0:T(8,128)(2,1)} %get-tuple-element.125, ...), kind=kOutput, calls=%fused_computation.8 | convolution fusion | flops 547880960 | bytes 11289088 | tf_op jit(solution)/shard_map/while/body/eval_jaxpr/cond/branch_0_fun/kgts,skd->kgtd/dot_general | solution.py:58
  149.5 1.0 copy-done.2
  150.4 0.2 copy.42
  150.6 2.9 %fusion.24 = bf16[256,2,4,128]{3,2,1,0:T(4,128)(2,1)} fusion(f32[2,4,256]{1,0,2:T(2,128)S(1)} %copy.42, f32[2,4,256,128]{3,2,1,0:T(8,128)} %get-tuple-element.142), kind=kLoop, calls=%fused_computation.31 | loop fusion | flops 524288 | bytes 1581056 | tf_op jit(solution)/shard_map/convert_element_type | solution.py:128
  (31 shorter events, 0.2 us)
Async XLA Ops:
  6.5 3.2 %copy-start = (bf16[256,1024]{1,0:T(8,128)(2,1)S(1)}, bf16[256,1024]{1,0:T(8,128)(2,1)}, u32[]{:S(2)}) copy-start(bf16[256,1024]{1,0:T(8,128)(2,1)} %param.16) | copy-start | bytes 1572868
  6.5 70.8 %all-gather.3.cloned.1.call-start = ((), (), s32[]{:S(2)}) async-start(), calls=%async_computation | async-start | bytes 1966080 | tf_op jit(solution)/shard_map/all_gather | solution.py:119
  40.7 74.2 %all-gather.5.cloned.1.call-start = ((), (), s32[]{:S(2)}) async-start(), calls=%async_computation.1 | async-start | bytes 1966080 | tf_op jit(solution)/shard_map/all_gather | solution.py:120
  120.7 3.5 %copy-start.1 = (f32[2,4,256,128]{3,2,1,0:T(8,128)S(1)}, f32[2,4,256,128]{3,2,1,0:T(8,128)}, u32[]{:S(2)}) copy-start(f32[2,4,256,128]{3,2,1,0:T(8,128)} %get-tuple-element.124) | copy-start | bytes 3145732 | tf_op jit(solution)/shard_map/while/body/eval_jaxpr/cond
  128.3 1.0 copy-start.2
  131.3 3.5 %copy-start.1 = (f32[2,4,256,128]{3,2,1,0:T(8,128)S(1)}, f32[2,4,256,128]{3,2,1,0:T(8,128)}, u32[]{:S(2)}) copy-start(f32[2,4,256,128]{3,2,1,0:T(8,128)} %get-tuple-element.124) | copy-start | bytes 3145732 | tf_op jit(solution)/shard_map/while/body/eval_jaxpr/cond
  138.9 1.0 copy-start.2
  141.9 3.5 %copy-start.1 = (f32[2,4,256,128]{3,2,1,0:T(8,128)S(1)}, f32[2,4,256,128]{3,2,1,0:T(8,128)}, u32[]{:S(2)}) copy-start(f32[2,4,256,128]{3,2,1,0:T(8,128)} %get-tuple-element.124) | copy-start | bytes 3145732 | tf_op jit(solution)/shard_map/while/body/eval_jaxpr/cond
  149.5 1.0 copy-start.2
Sparse Core Ops, SparseCore 0:
  40.8 36.4 all-gather.2
  78.9 35.9 all-gather.4
where the time goes:
time: 161 us; the launch traced here: 160 us
  waiting for transfers between devices  65.4 us (41%)
  blocking collectives  26 us (16%)
  matrix products  19.7 us (12%)
  between operations  16 us (10%)
  local copies, waits for them, and re-layouts  14.8 us (9%)
  other arithmetic  14.6 us (9%)
  loops' own time  3.9 us (2%)
    all_gather x1, waiting for transfers between devices, on_device(): value_piece = lax.all_gather(value_rows, 'blk', axis=0, tiled=True)  36 us
    all_gather x1, waiting for transfers between devices, on_device(): key_piece = lax.all_gather(key_rows, 'blk', axis=0, tiled=True)  29.3 us
    psum x1, blocking collectives, on_device(): latent = lax.psum(partial_latent, ('team', 'head')).astype(jnp.bfloat16)  26 us
    dot_general x3, matrix products, compute(): jnp.einsum('kgts,skd->kgtd', weights.astype(jnp.bfloat16), block_values,...  12.1 us
    unnamed x7, local copies, waits for them, and re-layouts  7.28 us
    reduce_sum x3, other arithmetic, compute(): row_sum = row_sum * factor + jnp.sum(weights, axis=-1)  6.09 us
    dot_general x3, matrix products, compute(): jnp.einsum('tkgd,skd->kgts', query_rows, block_keys, preferred_element_ty...  4.2 us
    another operation x1, loops' own time, attend(): result, _ = lax.scan(advance, running, (key_split, value_split, pos_split))  3.67 us
  transfers between devices with their start and end apart: 2, of which 2 were waited for; matrix products, arithmetic and copies ran while one was open for 5% of the time, Pallas kernels for 0%

commit v1 on v0

--- a/solution.py
+++ b/solution.py
@@ -1,3 +1,4 @@
+import functools
 import math
 import jax
 import jax.numpy as jnp
@@ -5,6 +6,14 @@
 from jax.sharding import PartitionSpec as P
 
 NEG_FILL = -1e30
+
+
+def place_members_all(message, axis_key):
+    frame_out = jnp.sum(lax.all_gather(message, axis_key), axis=0)
+    return frame_out
+
+
+words_touch = functools.partial(place_members_all, axis_key=("team", "head"))
 
 
 def block_length(row_count):
@@ -95,7 +104,7 @@
     chosen = adapter_ids[my_block]
     down_rows = lax.dynamic_index_in_dim(adapter_down, chosen, 0, keepdims=False)
     partial_latent = jnp.dot(features, down_rows, preferred_element_type=jnp.float32)
-    latent = lax.psum(partial_latent, ("team", "head")).astype(jnp.bfloat16)
+    latent = words_touch(partial_latent).astype(jnp.bfloat16)
 
     def expand(up_table, base_rows):
         up_rows = lax.dynamic_index_in_dim(up_table, chosen, 0, keepdims=False).reshape(

time: 161 us -> 148 us (0.919)
  blocking collectives: 26 us -> 11.3 us
    psum x1 -> x0, blocking collectives: 26 us -> none  [on_device(): latent = lax.psum(partial_latent, ('team', 'head')).astype(jnp.bfloat16)]
    all_gather x0 -> x1, blocking collectives: none -> 11.3 us  [place_members_all(): frame_out = jnp.sum(lax.all_gather(message, axis_key), axis=0)]
    unnamed x7 -> x8, local copies, waits for them, and re-layouts: 7.28 us -> 7.42 us
  transfers between devices with their start and end apart: 2 -> 2, of which waited for: 2 -> 2; matrix products, arithmetic and copies ran while one was open for 5% -> 6% of each run, Pallas kernels for 0% -> 0%
where the time goes in v1:
time: 148 us; the launch traced here: 147 us
  waiting for transfers between devices  66.1 us (45%)
  matrix products  19.7 us (13%)
  between operations  16 us (11%)
  local copies, waits for them, and re-layouts  14.9 us (10%)
  other arithmetic  14.8 us (10%)
  blocking collectives  11.3 us (8%)
  loops' own time  3.9 us (3%)
    all_gather x1, waiting for transfers between devices, on_device(): value_piece = lax.all_gather(value_rows, 'blk', axis=0, tiled=True)  36 us
    all_gather x1, waiting for transfers between devices, on_device(): key_piece = lax.all_gather(key_rows, 'blk', axis=0, tiled=True)  30.1 us
    dot_general x3, matrix products, compute(): jnp.einsum('kgts,skd->kgtd', weights.astype(jnp.bfloat16), block_values,...  12.1 us
    all_gather x1, blocking collectives, place_members_all(): frame_out = jnp.sum(lax.all_gather(message, axis_key), axis=0)  11.3 us
    unnamed x8, local copies, waits for them, and re-layouts  7.42 us
    reduce_sum x3, other arithmetic, compute(): row_sum = row_sum * factor + jnp.sum(weights, axis=-1)  6.09 us
    dot_general x3, matrix products, compute(): jnp.einsum('tkgd,skd->kgts', query_rows, block_keys, preferred_element_ty...  4.21 us
    another operation x1, loops' own time, attend(): result, _ = lax.scan(advance, running, (key_split, value_split, pos_split))  3.67 us
  transfers between devices with their start and end apart: 2, of which 2 were waited for; matrix products, arithmetic and copies ran while one was open for 6% of the time, Pallas kernels for 0%

profile of v1, /device:TPU:0, one launch (start us, length us, event | category | flops | bytes accessed | tf_op | source)
XLA Modules:
  0.0 146.8 jit_solution(10345011272907751840)
XLA Ops:
  6.5 1.3 dynamic_slice.39
  9.8 1.2 convolution_bitcast_fusion
  11.0 11.3 %all-gather = f32[2048,64]{0,1:T(8,128)S(1)} all-gather(f32[256,64]{0,1:T(8,128)S(1)} %convolution_bitcast_fusion), channel_id=2, replica_groups=mesh['team'=2,'blk'=4,'head'=4] {'team','head'}, dimensions={0}, use_global_device_ids=true | all-gather | bytes 589824 | tf_op jit(solution)/shard_map/all_gather | solution.py:12
  22.3 0.2 copy.49
  22.5 0.1 bitcast_reduce_fusion
  22.6 1.0 copy.35
  23.6 0.8 constant_dynamic-slice_fusion.1
  24.4 1.1 fusion.21
  25.6 0.8 pad_maximum_fusion
  26.3 0.0 all-gather.4.cloned.1.call-update
  26.4 0.0 all-gather.6.cloned.1.call-start
  26.4 1.0 copy.38
  27.4 1.1 fusion.22
  28.5 0.8 pad_maximum_fusion.1
  29.3 0.0 all-gather.6.cloned.1.call-update
  29.3 1.2 dynamic_slice.38
  31.1 0.6 add_reduce_fusion
  31.7 1.1 copy.40
  32.9 0.8 select_reduce_fusion
  33.7 30.1 %all-gather.4.cloned.1.call-done = bf16[3072,2,128]{2,0,1:T(8,128)(2,1)} async-done(((bf16[768,2,128]{2,0,1:T(8,128)(2,1)}), bf16[3072,2,128]{2,0,1:T(8,128)(2,1)}) %all-gather.4.cloned.1.call-update) | async-done | bytes 1572880 | tf_op jit(solution)/shard_map/all_gather | solution.py:128
  63.8 1.5 %copy.39 = bf16[3,1024,2,128]{3,1,2,0:T(8,128)(2,1)S(1)} copy(bf16[3,1024,2,128]{3,1,0,2:T(8,128)(2,1)} %bitcast.88) | data formatting | bytes 3145728
  65.4 36.0 %all-gather.6.cloned.1.call-done = bf16[3072,2,128]{2,0,1:T(8,128)(2,1)} async-done(((bf16[768,2,128]{2,0,1:T(8,128)(2,1)}), bf16[3072,2,128]{2,0,1:T(8,128)(2,1)}) %all-gather.6.cloned.1.call-update) | async-done | bytes 1572880 | tf_op jit(solution)/shard_map/all_gather | solution.py:129
  101.3 2.7 %copy.41 = bf16[3,1024,2,128]{3,1,2,0:T(8,128)(2,1)} copy(bf16[3,1024,2,128]{3,1,0,2:T(8,128)(2,1)} %bitcast.89) | data formatting | bytes 3145728
  104.0 1.0 broadcast_in_dim.56
  105.0 31.8 %while.15 = (s32[]{:T(128)}, f32[2,4,256]{2,1,0:T(4,128)S(1)}, f32[2,4,256]{2,1,0:T(4,128)S(1)}, f32[2,4,256,128]{3,2,1,0:T(8,128)}, s32[3,1024]{1,0:T(4,128)S(1...) while((s32[]{:T(128)}, f32[2,4,256]{2,1,0:T(4,128)S(1)}, ...), condition=%wide.region_9.10_spmd.clone, body=%wide.region_3.9_spmd.clone.sunk | while | flops 1101796608 | bytes 38421312 | solution.py:78
  105.0 0.6 fusion.45
  106.9 8.7 %conditional.3 = (f32[2,4,256]{2,1,0:T(4,128)S(1)}, f32[2,4,256]{2,1,0:T(4,128)S(1)}, f32[2,4,256,128]{3,2,1,0:T(8,128)}) conditional(s32[]{:T(128)} %convert_element_type.57, (s32[1,1024]{1,0:T(1,128)S(1)}, s32[]{:T(128)}, bf16[3,1024,2,128]{3,1,2,0:T(8,128)(2,1)S(1)}, s32[]{:T(128)}, bf16[256,2,4,128]{3,0,2,1:T(8,128)(2,1)S(1)}, ...), branch_computations={%region_5.7_spmd, %region_8.8_spmd} | conditional | flops 1101795584 | bytes 38395480 | solution.py:76
  106.9 0.2 broadcast_compare_fusion
  107.2 1.4 fusion.2
  108.6 2.0 %fusion.4 = f32[2,4,256]{2,1,0:T(4,128)S(1)} fusion(f32[2,1024,256,4]{2,1,3,0:T(8,128)S(1)} %get-tuple-element.228, f32[2,4,256]{2,1,0:T(4,128)S(1)} %max.4, pred[256,1024]{0,1:T(8,128)(4,1)S(1)} %broadcast_compare_fusion), kind=kLoop, calls=%fused_computation.5 | loop fusion | flops 10483712 | bytes 8667136 | tf_op jit(solution)/shard_map/while/body/eval_jaxpr/cond/branch_0_fun/reduce_sum | solution.py:66
  110.6 4.0 %fusion.8 = f32[2,4,256,128]{3,2,1,0:T(8,128)S(1)} fusion(f32[2,1024,256,4]{2,1,3,0:T(8,128)S(1)} %get-tuple-element.228, f32[2,4,256]{2,1,0:T(4,128)S(1)} %max.4, pred[256,1024]{0,1:T(8,128)(4,1)S(1)} %broadcast_compare_fusion, f32[2,4,256,128]{3,2,1,0:T(8,128)S(1)} %copy-done.1, bf16[3,1024,2,128]{3,1,2,0:T(8,128)(2,1)} %get-tuple-element.125, ...), kind=kOutput, calls=%fused_computation.8 | convolution fusion | flops 547880960 | bytes 11289088 | tf_op jit(solution)/shard_map/while/body/eval_jaxpr/cond/branch_0_fun/kgts,skd->kgtd/dot_general | solution.py:67
  114.7 1.0 copy-done.2
  115.6 0.6 fusion.45
  117.5 8.7 %conditional.3 = (f32[2,4,256]{2,1,0:T(4,128)S(1)}, f32[2,4,256]{2,1,0:T(4,128)S(1)}, f32[2,4,256,128]{3,2,1,0:T(8,128)}) conditional(s32[]{:T(128)} %convert_element_type.57, (s32[1,1024]{1,0:T(1,128)S(1)}, s32[]{:T(128)}, bf16[3,1024,2,128]{3,1,2,0:T(8,128)(2,1)S(1)}, s32[]{:T(128)}, bf16[256,2,4,128]{3,0,2,1:T(8,128)(2,1)S(1)}, ...), branch_computations={%region_5.7_spmd, %region_8.8_spmd} | conditional | flops 1101795584 | bytes 38395480 | solution.py:76
  117.5 0.2 broadcast_compare_fusion
  117.8 1.4 fusion.2
  119.2 2.0 %fusion.4 = f32[2,4,256]{2,1,0:T(4,128)S(1)} fusion(f32[2,1024,256,4]{2,1,3,0:T(8,128)S(1)} %get-tuple-element.228, f32[2,4,256]{2,1,0:T(4,128)S(1)} %max.4, pred[256,1024]{0,1:T(8,128)(4,1)S(1)} %broadcast_compare_fusion), kind=kLoop, calls=%fused_computation.5 | loop fusion | flops 10483712 | bytes 8667136 | tf_op jit(solution)/shard_map/while/body/eval_jaxpr/cond/branch_0_fun/reduce_sum | solution.py:66
  121.2 4.0 %fusion.8 = f32[2,4,256,128]{3,2,1,0:T(8,128)S(1)} fusion(f32[2,1024,256,4]{2,1,3,0:T(8,128)S(1)} %get-tuple-element.228, f32[2,4,256]{2,1,0:T(4,128)S(1)} %max.4, pred[256,1024]{0,1:T(8,128)(4,1)S(1)} %broadcast_compare_fusion, f32[2,4,256,128]{3,2,1,0:T(8,128)S(1)} %copy-done.1, bf16[3,1024,2,128]{3,1,2,0:T(8,128)(2,1)} %get-tuple-element.125, ...), kind=kOutput, calls=%fused_computation.8 | convolution fusion | flops 547880960 | bytes 11289088 | tf_op jit(solution)/shard_map/while/body/eval_jaxpr/cond/branch_0_fun/kgts,skd->kgtd/dot_general | solution.py:67
  125.3 1.0 copy-done.2
  126.2 0.6 fusion.45
  128.1 8.7 %conditional.3 = (f32[2,4,256]{2,1,0:T(4,128)S(1)}, f32[2,4,256]{2,1,0:T(4,128)S(1)}, f32[2,4,256,128]{3,2,1,0:T(8,128)}) conditional(s32[]{:T(128)} %convert_element_type.57, (s32[1,1024]{1,0:T(1,128)S(1)}, s32[]{:T(128)}, bf16[3,1024,2,128]{3,1,2,0:T(8,128)(2,1)S(1)}, s32[]{:T(128)}, bf16[256,2,4,128]{3,0,2,1:T(8,128)(2,1)S(1)}, ...), branch_computations={%region_5.7_spmd, %region_8.8_spmd} | conditional | flops 1101795584 | bytes 38395480 | solution.py:76
  128.1 0.2 broadcast_compare_fusion
  128.4 1.4 fusion.2
  129.8 2.0 %fusion.4 = f32[2,4,256]{2,1,0:T(4,128)S(1)} fusion(f32[2,1024,256,4]{2,1,3,0:T(8,128)S(1)} %get-tuple-element.228, f32[2,4,256]{2,1,0:T(4,128)S(1)} %max.4, pred[256,1024]{0,1:T(8,128)(4,1)S(1)} %broadcast_compare_fusion), kind=kLoop, calls=%fused_computation.5 | loop fusion | flops 10483712 | bytes 8667136 | tf_op jit(solution)/shard_map/while/body/eval_jaxpr/cond/branch_0_fun/reduce_sum | solution.py:66
  131.8 4.0 %fusion.8 = f32[2,4,256,128]{3,2,1,0:T(8,128)S(1)} fusion(f32[2,1024,256,4]{2,1,3,0:T(8,128)S(1)} %get-tuple-element.228, f32[2,4,256]{2,1,0:T(4,128)S(1)} %max.4, pred[256,1024]{0,1:T(8,128)(4,1)S(1)} %broadcast_compare_fusion, f32[2,4,256,128]{3,2,1,0:T(8,128)S(1)} %copy-done.1, bf16[3,1024,2,128]{3,1,2,0:T(8,128)(2,1)} %get-tuple-element.125, ...), kind=kOutput, calls=%fused_computation.8 | convolution fusion | flops 547880960 | bytes 11289088 | tf_op jit(solution)/shard_map/while/body/eval_jaxpr/cond/branch_0_fun/kgts,skd->kgtd/dot_general | solution.py:67
  135.9 1.0 copy-done.2
  136.8 0.2 copy.42
  137.0 2.9 %fusion.24 = bf16[256,2,4,128]{3,2,1,0:T(4,128)(2,1)} fusion(f32[2,4,256]{1,0,2:T(2,128)S(1)} %copy.42, f32[2,4,256,128]{3,2,1,0:T(8,128)} %get-tuple-element.142), kind=kLoop, calls=%fused_computation.32 | loop fusion | flops 524288 | bytes 1581056 | tf_op jit(solution)/shard_map/convert_element_type | solution.py:137
  (33 shorter events, 0.2 us)
Async XLA Ops:
  6.5 3.2 %copy-start = (bf16[256,1024]{1,0:T(8,128)(2,1)S(1)}, bf16[256,1024]{1,0:T(8,128)(2,1)}, u32[]{:S(2)}) copy-start(bf16[256,1024]{1,0:T(8,128)(2,1)} %param.16) | copy-start | bytes 1572868
  6.5 57.3 %all-gather.4.cloned.1.call-start = ((), (), s32[]{:S(2)}) async-start(), calls=%async_computation | async-start | bytes 1966080 | tf_op jit(solution)/shard_map/all_gather | solution.py:128
  26.4 75.0 %all-gather.6.cloned.1.call-start = ((), (), s32[]{:S(2)}) async-start(), calls=%async_computation.1 | async-start | bytes 1966080 | tf_op jit(solution)/shard_map/all_gather | solution.py:129
  107.1 3.5 %copy-start.1 = (f32[2,4,256,128]{3,2,1,0:T(8,128)S(1)}, f32[2,4,256,128]{3,2,1,0:T(8,128)}, u32[]{:S(2)}) copy-start(f32[2,4,256,128]{3,2,1,0:T(8,128)} %get-tuple-element.124) | copy-start | bytes 3145732 | tf_op jit(solution)/shard_map/while/body/eval_jaxpr/cond
  114.7 1.0 copy-start.2
  117.7 3.5 %copy-start.1 = (f32[2,4,256,128]{3,2,1,0:T(8,128)S(1)}, f32[2,4,256,128]{3,2,1,0:T(8,128)}, u32[]{:S(2)}) copy-start(f32[2,4,256,128]{3,2,1,0:T(8,128)} %get-tuple-element.124) | copy-start | bytes 3145732 | tf_op jit(solution)/shard_map/while/body/eval_jaxpr/cond
  125.3 1.0 copy-start.2
  128.4 3.5 %copy-start.1 = (f32[2,4,256,128]{3,2,1,0:T(8,128)S(1)}, f32[2,4,256,128]{3,2,1,0:T(8,128)}, u32[]{:S(2)}) copy-start(f32[2,4,256,128]{3,2,1,0:T(8,128)} %get-tuple-element.124) | copy-start | bytes 3145732 | tf_op jit(solution)/shard_map/while/body/eval_jaxpr/cond
  135.9 1.0 copy-start.2
Sparse Core Ops, SparseCore 0:
  26.5 37.3 all-gather.3
  65.4 35.8 all-gather.5
